TPU v7x, 512 devices: a whole 4x4x16 slice. The times are simulated.
512 devices in a mesh: blk: 32 (over x, z_lo), rep: 16 (over z_hi, y, core).
Axes of the slice: x: 4, y: 4, z: 16 (z_hi: 2, z_lo: 8; z = z_hi * 8 + z_lo), core: 2. Of those that a mesh axis runs over, the one named last changes fastest.
Arguments:
- signals: bfloat16 [32768, 8192], P('rep', 'blk'), may hold values from -6 to 6
- omega: float32 [32, 5, 256, 256], P('blk', None, 'rep'), may hold values from -1.2 to 3, as said below
- pattern: int32 [32, 5], P('blk'), may hold values from 0 to 31, as said below
Outputs:
- omega_next: float32 [32, 5, 256, 256], P('blk', None, 'rep')
Inputs may be any that keep to these rules, and one draw needn't show every extreme that they name: pattern[i, 0] = i. For two distinct whole numbers A and B from 1 to 15, the same in every row, pattern[i, 1] to pattern[i, 4] are i + A, i - A, i + B and i - B modulo 32 in some order, the same order in every row. Omega is symmetric: omega[i, k] is the transpose of omega[pattern[i, k], k2] where pattern[pattern[i, k], k2] = i. The diagonal entries of omega[i, 0] lie between 1 and 3.
All inputs are finite; a program needn't handle non-finite values.
Results may differ from a plain program's by a relative error of at most 0.0033.
Values may be sent and summed in bfloat16 or wider, within the bound.
A program may use at most 128 MiB of HBM per device.

v0:
```python
import jax
import jax.numpy as jnp
from jax import lax
from jax.sharding import Mesh
from jax.sharding import PartitionSpec as P

STEP_SIZE = 0.5
PENALTY = 0.1
REP = ("zh", "y", "c")


def fine_mesh(mesh):
    return Mesh(mesh.devices.reshape(4, 8, 2, 4, 2), ("x", "zl", "zh", "y", "c"))


def per_device(signals, omega, pattern):
    x_size = lax.axis_size("x")
    zl_size = lax.axis_size("zl")
    team_count = x_size * zl_size
    replica_count = lax.axis_size(REP)
    team_index = lax.axis_index(("x", "zl"))
    replica_index = lax.axis_index(REP)
    slot_count, tile_rows, width = omega.shape[1:]
    time_length = signals.shape[0] * replica_count
    offsets = jnp.mod(pattern[0] - team_index, team_count)
    own = signals.reshape(zl_size, signals.shape[0] // zl_size, width)
    blocks = lax.all_to_all(own, "zl", 0, 0, tiled=True)
    blocks = lax.all_gather(blocks, "x", axis=0, tiled=True)
    panels = lax.all_gather(omega.astype(jnp.bfloat16), REP, axis=2, tiled=True)
    panels = lax.all_gather(panels, "zl", axis=0, tiled=True)
    rows = lax.axis_index("x") * zl_size + jnp.arange(zl_size, dtype=jnp.int32)
    columns = jnp.mod(rows[:, None] + offsets[None, :], team_count)
    gathered = blocks[columns]
    mixed = jnp.einsum(
        "jktc,jkdc->jtd", gathered, panels, preferred_element_type=jnp.float32
    ).astype(jnp.bfloat16)
    left = jnp.einsum("jtd,jktc->jkdc", mixed, gathered, preferred_element_type=jnp.float32)
    own_terms = lax.psum_scatter(left, REP, scatter_dimension=2, tiled=True)
    own_terms = lax.psum_scatter(own_terms, "zl", scatter_dimension=0, tiled=True)[0]
    flipped = lax.all_to_all(own_terms, REP, 2, 1, tiled=True)
    flipped = jnp.swapaxes(flipped, 1, 2)
    match = offsets[None, :] == jnp.mod(team_count - offsets, team_count)[:, None]
    mirror = jnp.argmax(match, axis=1)
    outgoing = flipped[mirror]
    for level in range(team_count.bit_length() - 1):
        step = 1 << level
        route = [((i + step) % team_count, i) for i in range(team_count)]
        shifted = lax.ppermute(outgoing, ("x", "zl"), route)
        chosen = jnp.mod(offsets // step, 2) == 1
        outgoing = jnp.where(chosen[:, None, None], shifted, outgoing)
    gradient = (own_terms + outgoing) / (2.0 * time_length)
    tiles = omega[0]
    column_ids = jnp.arange(width, dtype=jnp.int32)
    row_ids = replica_index * tile_rows + jnp.arange(tile_rows, dtype=jnp.int32)
    diagonal = column_ids[None, :] == row_ids[:, None]
    diagonal = diagonal[None] & (offsets == 0)[:, None, None]
    gradient = gradient - jnp.where(diagonal, 1.0 / jnp.where(diagonal, tiles, 1.0), 0.0)
    value = tiles - STEP_SIZE * gradient
    shrunk = jnp.sign(value) * jnp.maximum(jnp.abs(value) - STEP_SIZE * PENALTY, 0.0)
    return jnp.where(diagonal, value, shrunk)[None]


def solution(mesh):
    return jax.shard_map(
        per_device,
        mesh=fine_mesh(mesh),
        in_specs=(P(REP, ("x", "zl")), P(("x", "zl"), None, REP, None), P(("x", "zl"), None)),
        out_specs=P(("x", "zl"), None, REP, None),
        check_vma=False,
    )
```

profile of v0, /device:TPU:230, one launch (start us, length us, event | category | flops | bytes accessed | tf_op | source)
XLA Modules:
  0.0 669.5 jit_solution(8638916152552195182)
XLA Ops:
  6.5 55.6 %all_to_all.23 = bf16[8,256,256]{2,1,0:T(8,128)(2,1)} all-to-all(bf16[8,256,256]{2,1,0:T(8,128)(2,1)} %bitcast.50), channel_id=1, replica_groups=mesh['x'=4,'zl'=8,'zh'=2,'y'=4,'c'=2] {'zl'}, dimensions={0} | all-to-all | bytes 2097152 | tf_op jit(solution)/shard_map/all_to_all | solution.py:27
  63.1 45.3 %all_gather.10 = bf16[1,5,256,256]{3,2,1,0:T(8,128)(2,1)} all-gather(bf16[1,5,16,256]{3,2,1,0:T(8,128)(2,1)S(1)} %convert_element_type.6), channel_id=1, replica_groups=mesh['x'=4,'zl'=8,'zh'=2,'y'=4,'c'=2] {'zh','y','c'}, dimensions={2}, use_global_device_ids=true | all-gather | bytes 696320 | tf_op jit(solution)/shard_map/all_gather | solution.py:29
  109.3 10.0 %all-gather.3.cloned.1.call-done = bf16[32,256,256]{2,1,0:T(8,128)(2,1)} async-done(((bf16[8,256,256]{2,1,0:T(8,128)(2,1)}), bf16[32,256,256]{2,1,0:T(8,128)(2,1)}) %all-gather.3.cloned.1.call-update) | async-done | bytes 4194320 | tf_op jit(solution)/shard_map/all_gather | solution.py:28
  119.3 6.7 %gather_fusion = bf16[40,256,256]{2,1,0:T(8,128)(2,1)} fusion(bf16[32,256,256]{2,1,0:T(8,128)(2,1)} %all-gather.3.cloned.1.call-done, s32[1024]{0:T(1024)S(1)} %pad_clamp_fusion.1), kind=kCustom, calls=%fused_computation | custom fusion | bytes 10485920 | tf_op jit(solution)/shard_map/gather | solution.py:33
  126.0 114.0 %all-gather.5.cloned.1.call-done = bf16[8,5,256,256]{3,2,1,0:T(8,128)(2,1)} async-done(((bf16[1,5,256,256]{3,2,1,0:T(8,128)(2,1)}), bf16[8,5,256,256]{3,2,1,0:T(8,128)(2,1)}) %all-gather.5.cloned.1.call-update) | async-done | bytes 5242896 | tf_op jit(solution)/shard_map/all_gather | solution.py:30
  240.0 12.5 %convolution_bitcast_fusion = f32[8,5,256,256]{2,3,1,0:T(8,128)} fusion(bf16[8,5,256,256]{3,2,1,0:T(8,128)(2,1)} %bitcast.46, bf16[8,5,256,256]{3,2,1,0:T(8,128)(2,1)} %all-gather.5.cloned.1.call-done), kind=kOutput, calls=%fused_computation.2 | convolution fusion | flops 2684878848 | bytes 20971520 | tf_op jit(solution)/shard_map/jtd,jktc->jkdc/dot_general | solution.py:37
  252.5 11.6 %copy.24 = f32[8,5,256,256]{3,0,1,2:T(8,128)} copy(f32[8,5,256,256]{2,3,1,0:T(8,128)} %convolution_bitcast_fusion) | data formatting | bytes 20971520 | tf_op jit(solution)/shard_map/jtd,jktc->jkdc/transpose | solution.py:37
  264.2 245.1 %reduce-scatter.3.cloned.1.call-done = f32[8,5,16,256]{3,0,1,2:T(8,128)} async-done(((f32[8,5,256,256]{3,0,1,2:T(8,128)}), f32[8,5,16,256]{3,0,1,2:T(8,128)}) %reduce-scatter.3.cloned.1.call-update) | async-done | bytes 655376 | tf_op jit(solution)/shard_map/reduce_scatter | solution.py:38
  509.3 2.1 copy.25
  512.2 58.2 %reduce-scatter.5.cloned.1.call-done = f32[1,5,16,256]{3,2,1,0:T(8,128)} async-done(((f32[8,5,16,256]{3,2,1,0:T(8,128)}), f32[1,5,16,256]{3,2,1,0:T(8,128)}) %reduce-scatter.5.cloned.1.call-update) | async-done | bytes 81936 | tf_op jit(solution)/shard_map/reduce_scatter | solution.py:39
  570.4 1.4 copy.26
  571.8 1.0 reshape.312
  572.8 14.2 %all-to-all-start.1 = ((f32[16,1,1280]{2,1,0:T(1,128)}), f32[16,1,1280]{2,1,0:T(1,128)S(1)}, u32[]{:S(2)}, u32[]{:S(2)}) async-start(f32[16,1,1280]{2,1,0:T(1,128)} %reshape.312), calls=%async_computation.3 | async-start | bytes 163840 | tf_op jit(solution)/shard_map/all_to_all | solution.py:40
  587.0 15.0 %all-to-all-done.1 = f32[16,1,1280]{2,1,0:T(1,128)S(1)} async-done(((f32[16,1,1280]{2,1,0:T(1,128)}), f32[16,1,1280]{2,1,0:T(1,128)S(1)}, u32[]{:S(2)}, u32[]{:S(2)}) %all-to-all-start.1) | async-done | bytes 81952 | tf_op jit(solution)/shard_map/all_to_all | solution.py:40
  604.9 1.9 collective-permute-start
  606.9 13.1 %collective-permute-done = f32[5,16,256]{2,1,0:T(8,128)S(1)} collective-permute-done((f32[5,16,256]{2,1,0:T(8,128)S(1)}, f32[5,16,256]{2,1,0:T(8,128)S(1)}, u32[]{:S(2)}, u32[]{:S(2)}) %collective-permute-start) | collective-permute-done | bytes 81952 | tf_op jit(solution)/shard_map/ppermute | solution.py:48
  620.1 1.9 collective-permute-start.1
  622.0 12.3 %collective-permute-done.1 = f32[5,16,256]{2,1,0:T(8,128)S(1)} collective-permute-done((f32[5,16,256]{2,1,0:T(8,128)S(1)}, f32[5,16,256]{2,1,0:T(8,128)S(1)}, u32[]{:S(2)}, u32[]{:S(2)}) %collective-permute-start.1) | collective-permute-done | bytes 81952 | tf_op jit(solution)/shard_map/ppermute | solution.py:48
  634.3 1.9 collective-permute-start.2
  636.2 10.4 %collective-permute-done.2 = f32[5,16,256]{2,1,0:T(8,128)S(1)} collective-permute-done((f32[5,16,256]{2,1,0:T(8,128)S(1)}, f32[5,16,256]{2,1,0:T(8,128)S(1)}, u32[]{:S(2)}, u32[]{:S(2)}) %collective-permute-start.2) | collective-permute-done | bytes 81952 | tf_op jit(solution)/shard_map/ppermute | solution.py:48
  646.7 1.9 collective-permute-start.3
  648.7 5.6 collective-permute-done.3
  654.3 1.9 collective-permute-start.4
  656.3 5.8 collective-permute-done.4
  (39 shorter events, 6.8 us)
Async XLA Ops:
  6.5 112.7 %all-gather.3.cloned.1.call-start = ((), (), s32[]{:S(2)}) async-start(), calls=%async_computation.4 | async-start | bytes 5242880 | tf_op jit(solution)/shard_map/all_gather | solution.py:28
  62.1 177.9 %all-gather.5.cloned.1.call-start = ((), (), s32[]{:S(2)}) async-start(), calls=%async_computation.5 | async-start | bytes 5898240 | tf_op jit(solution)/shard_map/all_gather | solution.py:30
  108.4 400.9 %reduce-scatter.3.cloned.1.call-start = ((), (), s32[]{:S(2)}) async-start(), calls=%async_computation.6 | async-start | bytes 11141120 | tf_op jit(solution)/shard_map/reduce_scatter | solution.py:38
  264.1 247.4 %copy-start.2 = (s32[1,5]{1,0:T(1,128)S(1)}, s32[1,5]{1,0:T(1,128)}, u32[]{:S(2)}) copy-start(s32[1,5]{1,0:T(1,128)} %param.5) | copy-start | bytes 64
  264.2 398.0 %copy-start.1 = (f32[1,5,16,256]{3,2,1,0:T(8,128)S(1)}, f32[1,5,16,256]{3,2,1,0:T(8,128)}, u32[]{:S(2)}) copy-start(f32[1,5,16,256]{3,2,1,0:T(8,128)} %param.4) | copy-start | bytes 245764
  264.2 306.2 %reduce-scatter.5.cloned.1.call-start = ((), (), s32[]{:S(2)}) async-start(), calls=%async_computation.7 | async-start | bytes 737280 | tf_op jit(solution)/shard_map/reduce_scatter | solution.py:39
  570.4 91.8 %copy-start = (f32[1,5,16,256]{3,2,1,0:T(8,128)S(1)}, f32[1,5,16,256]{3,2,1,0:T(8,128)}, u32[]{:S(2)}) copy-start(f32[1,5,16,256]{3,2,1,0:T(8,128)} %reduce-scatter.5.cloned.1.call-done) | copy-start | bytes 245764
  572.8 29.2 %all-to-all-start.1 = ((f32[16,1,1280]{2,1,0:T(1,128)}), f32[16,1,1280]{2,1,0:T(1,128)S(1)}, u32[]{:S(2)}, u32[]{:S(2)}) async-start(f32[16,1,1280]{2,1,0:T(1,128)} %reshape.312), calls=%async_computation.3 | async-start | bytes 163840 | tf_op jit(solution)/shard_map/all_to_all | solution.py:40
  604.9 15.0 %collective-permute-start = (f32[5,16,256]{2,1,0:T(8,128)S(1)}, f32[5,16,256]{2,1,0:T(8,128)S(1)}, u32[]{:S(2)}, u32[]{:S(2)}) collective-permute-start(f32[5,16,256]{2,1,0:T(8,128)S(1)} %gather_fusion.1), channel_id=1, source_target_pairs={{16,0},{32,16},{48,32},{64,48},{80,64},{96,80},{112,96},{128,112},... | collective-permute-start | bytes 245768 | tf_op jit(solution)/shard_map/ppermute | solution.py:48
  620.1 14.2 %collective-permute-start.1 = (f32[5,16,256]{2,1,0:T(8,128)S(1)}, f32[5,16,256]{2,1,0:T(8,128)S(1)}, u32[]{:S(2)}, u32[]{:S(2)}) collective-permute-start(f32[5,16,256]{2,1,0:T(8,128)S(1)} %broadcast_select_fusion), channel_id=1, source_target_pairs={{32,0},{48,16},{64,32},{80,48},{96,64},{112,80},{128,96},{144,112}... | collective-permute-start | bytes 245768 | tf_op jit(solution)/shard_map/ppermute | solution.py:48
  634.3 12.3 %collective-permute-start.2 = (f32[5,16,256]{2,1,0:T(8,128)S(1)}, f32[5,16,256]{2,1,0:T(8,128)S(1)}, u32[]{:S(2)}, u32[]{:S(2)}) collective-permute-start(f32[5,16,256]{2,1,0:T(8,128)S(1)} %broadcast_select_fusion.1), channel_id=1, source_target_pairs={{64,0},{80,16},{96,32},{112,48},{128,64},{144,80},{160,96},{176,11... | collective-permute-start | bytes 245768 | tf_op jit(solution)/shard_map/ppermute | solution.py:48
  646.7 7.5 %collective-permute-start.3 = (f32[5,16,256]{2,1,0:T(8,128)S(1)}, f32[5,16,256]{2,1,0:T(8,128)S(1)}, u32[]{:S(2)}, u32[]{:S(2)}) collective-permute-start(f32[5,16,256]{2,1,0:T(8,128)S(1)} %broadcast_select_fusion.2), channel_id=1, source_target_pairs={{128,0},{144,16},{160,32},{176,48},{192,64},{208,80},{224,96},{240... | collective-permute-start | bytes 245768 | tf_op jit(solution)/shard_map/ppermute | solution.py:48
  654.3 7.8 %collective-permute-start.4 = (f32[5,16,256]{2,1,0:T(8,128)S(1)}, f32[5,16,256]{2,1,0:T(8,128)S(1)}, u32[]{:S(2)}, u32[]{:S(2)}) collective-permute-start(f32[5,16,256]{2,1,0:T(8,128)S(1)} %broadcast_select_fusion.3), channel_id=1, source_target_pairs={{256,0},{272,16},{288,32},{304,48},{320,64},{336,80},{352,96},{368... | collective-permute-start | bytes 245768 | tf_op jit(solution)/shard_map/ppermute | solution.py:48
Sparse Core Ops, SparseCore 0:
  62.2 56.9 all-gather.2
  121.4 118.6 all-gather.4
  264.3 245.0 reduce-scatter.2
  512.3 58.1 reduce-scatter.4
where the time goes:
time: 670 us; the launch traced here: 669 us
  waiting for transfers between devices  490 us (73%)
  blocking collectives  101 us (15%)
  local copies, waits for them, and re-layouts  25 us (4%)
  starting transfers between devices  23.9 us (4%)
  between operations  13.3 us (2%)
  matrix products  12.5 us (2%)
    reduce_scatter x1, waiting for transfers between devices, per_device(): own_terms = lax.psum_scatter(left, REP, scatter_dimension=2, tiled=True)  245 us
    all_gather x1, waiting for transfers between devices, per_device(): panels = lax.all_gather(panels, 'zl', axis=0, tiled=True)  114 us
    reduce_scatter x1, waiting for transfers between devices, per_device(): lax.psum_scatter(own_terms, 'zl', scatter_dimension=0, tiled=True)[0]  58.2 us
    all_to_all x1, blocking collectives, per_device(): blocks = lax.all_to_all(own, 'zl', 0, 0, tiled=True)  55.6 us
    ppermute x5, waiting for transfers between devices, per_device(): shifted = lax.ppermute(outgoing, ('x', 'zl'), route)  47.2 us
    all_gather x1, blocking collectives, per_device(): panels = lax.all_gather(omega.astype(jnp.bfloat16), REP, axis=2, tiled=True)  45.3 us
    all_to_all x1, waiting for transfers between devices, per_device(): flipped = lax.all_to_all(own_terms, REP, 2, 1, tiled=True)  15 us
    all_to_all x1, starting transfers between devices, per_device(): flipped = lax.all_to_all(own_terms, REP, 2, 1, tiled=True)  14.2 us
  transfers between devices with their start and end apart: 10, of which 10 were waited for; matrix products, arithmetic and copies ran while one was open for 1% of the time, Pallas kernels for 0%

commit v1 on v0

--- a/solution.py
+++ b/solution.py
@@ -27,7 +27,9 @@
     blocks = lax.all_to_all(own, "zl", 0, 0, tiled=True)
     blocks = lax.all_gather(blocks, "x", axis=0, tiled=True)
     panels = lax.all_gather(omega.astype(jnp.bfloat16), REP, axis=2, tiled=True)
-    panels = lax.all_gather(panels, "zl", axis=0, tiled=True)
+    panels = jnp.concatenate(
+        lax.all_to_all(jnp.stack([panels] * lax.axis_size("zl")), "zl", 0, 0), axis=0
+    )
     rows = lax.axis_index("x") * zl_size + jnp.arange(zl_size, dtype=jnp.int32)
     columns = jnp.mod(rows[:, None] + offsets[None, :], team_count)
     gathered = blocks[columns]

time: 670 us -> 766 us (1.14)
  waiting for transfers between devices: 490 us -> 583 us
  blocking collectives: 101 us -> 54.6 us
  starting transfers between devices: 23.9 us -> 70.2 us
    all_to_all x0 -> x2, waiting for transfers between devices: none -> 165 us  [the longest x1 165 us: per_device(): lax.all_to_all(jnp.stack([panels] * lax.axis_size('zl')), 'zl', 0, 0)]
    all_gather x1 -> x0, waiting for transfers between devices: 114 us -> none  [per_device(): panels = lax.all_gather(panels, 'zl', axis=0, tiled=True)]
    all_to_all x1 -> x0, blocking collectives: 55.6 us -> none  [per_device(): blocks = lax.all_to_all(own, 'zl', 0, 0, tiled=True)]
    all_to_all x0 -> x2, starting transfers between devices: none -> 46.4 us  [the longest x1 36.5 us: per_device(): lax.all_to_all(jnp.stack([panels] * lax.axis_size('zl')), 'zl', 0, 0)]
    all_gather x1, waiting for transfers between devices: 9.95 us -> 53 us  [per_device(): blocks = lax.all_gather(blocks, 'x', axis=0, tiled=True)]
    all_gather x1, blocking collectives: 45.3 us -> 54.6 us  [per_device(): panels = lax.all_gather(omega.astype(jnp.bfloat16), REP, axis=2, tiled=True)]
  transfers between devices with their start and end apart: 10 -> 11, of which waited for: 10 -> 10; matrix products, arithmetic and copies ran while one was open for 1% -> 1% of each run, Pallas kernels for 0% -> 0%
where the time goes in v1:
time: 766 us; the launch traced here: 765 us
  waiting for transfers between devices  583 us (76%)
  starting transfers between devices  70.2 us (9%)
  blocking collectives  54.6 us (7%)
  local copies, waits for them, and re-layouts  27.9 us (4%)
  between operations  13.3 us (2%)
  matrix products  12.5 us (2%)
    reduce_scatter x1, waiting for transfers between devices, per_device(): own_terms = lax.psum_scatter(left, REP, scatter_dimension=2, tiled=True)  243 us
    all_to_all x1, waiting for transfers between devices, per_device(): lax.all_to_all(jnp.stack([panels] * lax.axis_size('zl')), 'zl', 0, 0)  165 us
    reduce_scatter x1, waiting for transfers between devices, per_device(): lax.psum_scatter(own_terms, 'zl', scatter_dimension=0, tiled=True)[0]  58.4 us
    all_gather x1, blocking collectives, per_device(): panels = lax.all_gather(omega.astype(jnp.bfloat16), REP, axis=2, tiled=True)  54.6 us
    all_gather x1, waiting for transfers between devices, per_device(): blocks = lax.all_gather(blocks, 'x', axis=0, tiled=True)  53 us
    ppermute x5, waiting for transfers between devices, per_device(): shifted = lax.ppermute(outgoing, ('x', 'zl'), route)  47.2 us
    all_to_all x1, starting transfers between devices, per_device(): lax.all_to_all(jnp.stack([panels] * lax.axis_size('zl')), 'zl', 0, 0)  36.5 us
  transfers between devices with their start and end apart: 11, of which 10 were waited for; matrix products, arithmetic and copies ran while one was open for 1% of the time, Pallas kernels for 0%

profile of v1, /device:TPU:230, one launch (start us, length us, event | category | flops | bytes accessed | tf_op | source)
XLA Modules:
  0.0 765.0 jit_solution(1344722893748260345)
XLA Ops:
  6.5 9.9 %all-to-all-start = ((bf16[8,256,256]{2,1,0:T(8,128)(2,1)}), bf16[8,256,256]{2,1,0:T(8,128)(2,1)S(1)}, u32[]{:S(2)}, u32[]{:S(2)}) async-start(bf16[8,256,256]{2,1,0:T(8,128)(2,1)} %bitcast.60), calls=%async_computation | async-start | bytes 2097152 | tf_op jit(solution)/shard_map/all_to_all | solution.py:27
  17.3 54.6 %all_gather.9 = bf16[1,5,256,256]{3,2,1,0:T(8,128)(2,1)S(1)} all-gather(bf16[1,5,16,256]{3,2,1,0:T(8,128)(2,1)S(1)} %convert_element_type.6), channel_id=1, replica_groups=mesh['x'=4,'zl'=8,'zh'=2,'y'=4,'c'=2] {'zh','y','c'}, dimensions={2}, use_global_device_ids=true | all-gather | bytes 696320 | tf_op jit(solution)/shard_map/all_gather | solution.py:29
  72.0 2.9 stack.2
  74.9 36.5 %all-to-all-start.1 = ((bf16[8,1,5,256,256]{4,3,2,1,0:T(8,128)(2,1)}), bf16[8,1,5,256,256]{4,3,2,1,0:T(8,128)(2,1)}, u32[]{:S(2)}, u32[]{:S(2)}) async-start(bf16[8,1,5,256,256]{4,3,2,1,0:T(8,128)(2,1)} %stack.2), calls=%async_computation.1 | async-start | bytes 10485760 | tf_op jit(solution)/shard_map/all_to_all | solution.py:31
  112.3 53.0 %all-gather.2.cloned.1.call-done = bf16[32,256,256]{2,1,0:T(8,128)(2,1)} async-done(((bf16[8,256,256]{2,1,0:T(8,128)(2,1)}), bf16[32,256,256]{2,1,0:T(8,128)(2,1)}) %all-gather.2.cloned.1.call-update) | async-done | bytes 4194320 | tf_op jit(solution)/shard_map/all_gather | solution.py:28
  165.4 6.7 gather_fusion
  172.1 165.3 %all-to-all-done.1 = bf16[8,1,5,256,256]{4,3,2,1,0:T(8,128)(2,1)} async-done(((bf16[8,1,5,256,256]{4,3,2,1,0:T(8,128)(2,1)}), bf16[8,1,5,256,256]{4,3,2,1,0:T(8,128)(2,1)}, u32[]{:S(2)}, u32[]{:S(2)}) %all-to-all-start.1) | async-done | bytes 5242912 | tf_op jit(solution)/shard_map/all_to_all | solution.py:31
  337.3 12.5 %convolution_bitcast_fusion = f32[8,5,256,256]{2,3,1,0:T(8,128)} fusion(bf16[8,5,256,256]{3,2,1,0:T(8,128)(2,1)} %bitcast.55, bf16[8,1,5,256,256]{4,3,2,1,0:T(8,128)(2,1)} %all-to-all-done.1), kind=kOutput, calls=%fused_computation.4 | convolution fusion | flops 2684878848 | bytes 20971520 | tf_op jit(solution)/shard_map/jtd,jktc->jkdc/dot_general | solution.py:39
  349.8 11.6 %copy.24 = f32[8,5,256,256]{3,0,1,2:T(8,128)} copy(f32[8,5,256,256]{2,3,1,0:T(8,128)} %convolution_bitcast_fusion) | data formatting | bytes 20971520 | tf_op jit(solution)/shard_map/jtd,jktc->jkdc/transpose | solution.py:39
  361.5 243.2 %reduce-scatter.3.cloned.1.call-done = f32[8,5,16,256]{3,0,1,2:T(8,128)} async-done(((f32[8,5,256,256]{3,0,1,2:T(8,128)}), f32[8,5,16,256]{3,0,1,2:T(8,128)}) %reduce-scatter.3.cloned.1.call-update) | async-done | bytes 655376 | tf_op jit(solution)/shard_map/reduce_scatter | solution.py:40
  604.6 2.1 copy.25
  607.5 58.4 %reduce-scatter.5.cloned.1.call-done = f32[1,5,16,256]{3,2,1,0:T(8,128)} async-done(((f32[8,5,16,256]{3,2,1,0:T(8,128)}), f32[1,5,16,256]{3,2,1,0:T(8,128)}) %reduce-scatter.5.cloned.1.call-update) | async-done | bytes 81936 | tf_op jit(solution)/shard_map/reduce_scatter | solution.py:41
  668.3 14.2 %all-to-all-start.2 = ((f32[16,1,1280]{2,1,0:T(1,128)}), f32[16,1,1280]{2,1,0:T(1,128)S(1)}, u32[]{:S(2)}, u32[]{:S(2)}) async-start(f32[16,1,1280]{2,1,0:T(1,128)} %reshape.319), calls=%async_computation.4 | async-start | bytes 163840 | tf_op jit(solution)/shard_map/all_to_all | solution.py:42
  682.5 15.0 %all-to-all-done.2 = f32[16,1,1280]{2,1,0:T(1,128)S(1)} async-done(((f32[16,1,1280]{2,1,0:T(1,128)}), f32[16,1,1280]{2,1,0:T(1,128)S(1)}, u32[]{:S(2)}, u32[]{:S(2)}) %all-to-all-start.2) | async-done | bytes 81952 | tf_op jit(solution)/shard_map/all_to_all | solution.py:42
  700.5 1.9 collective-permute-start
  702.4 13.1 %collective-permute-done = f32[5,16,256]{2,1,0:T(8,128)S(1)} collective-permute-done((f32[5,16,256]{2,1,0:T(8,128)S(1)}, f32[5,16,256]{2,1,0:T(8,128)S(1)}, u32[]{:S(2)}, u32[]{:S(2)}) %collective-permute-start) | collective-permute-done | bytes 81952 | tf_op jit(solution)/shard_map/ppermute | solution.py:50
  715.6 1.9 collective-permute-start.1
  717.5 12.3 %collective-permute-done.1 = f32[5,16,256]{2,1,0:T(8,128)S(1)} collective-permute-done((f32[5,16,256]{2,1,0:T(8,128)S(1)}, f32[5,16,256]{2,1,0:T(8,128)S(1)}, u32[]{:S(2)}, u32[]{:S(2)}) %collective-permute-start.1) | collective-permute-done | bytes 81952 | tf_op jit(solution)/shard_map/ppermute | solution.py:50
  729.8 1.9 collective-permute-start.2
  731.8 10.4 %collective-permute-done.2 = f32[5,16,256]{2,1,0:T(8,128)S(1)} collective-permute-done((f32[5,16,256]{2,1,0:T(8,128)S(1)}, f32[5,16,256]{2,1,0:T(8,128)S(1)}, u32[]{:S(2)}, u32[]{:S(2)}) %collective-permute-start.2) | collective-permute-done | bytes 81952 | tf_op jit(solution)/shard_map/ppermute | solution.py:50
  742.2 1.9 collective-permute-start.3
  744.2 5.6 collective-permute-done.3
  749.9 1.9 collective-permute-start.4
  751.9 5.8 collective-permute-done.4
  (42 shorter events, 9.1 us)
Async XLA Ops:
  6.5 65.4 %all-to-all-start = ((bf16[8,256,256]{2,1,0:T(8,128)(2,1)}), bf16[8,256,256]{2,1,0:T(8,128)(2,1)S(1)}, u32[]{:S(2)}, u32[]{:S(2)}) async-start(bf16[8,256,256]{2,1,0:T(8,128)(2,1)} %bitcast.60), calls=%async_computation | async-start | bytes 2097152 | tf_op jit(solution)/shard_map/all_to_all | solution.py:27
  72.0 2.9 copy-start
  74.9 37.3 %copy-start.3 = (s32[1,5]{1,0:T(1,128)S(1)}, s32[1,5]{1,0:T(1,128)}, u32[]{:S(2)}) copy-start(s32[1,5]{1,0:T(1,128)} %param.5) | copy-start | bytes 64
  74.9 262.4 %all-to-all-start.1 = ((bf16[8,1,5,256,256]{4,3,2,1,0:T(8,128)(2,1)}), bf16[8,1,5,256,256]{4,3,2,1,0:T(8,128)(2,1)}, u32[]{:S(2)}, u32[]{:S(2)}) async-start(bf16[8,1,5,256,256]{4,3,2,1,0:T(8,128)(2,1)} %stack.2), calls=%async_computation.1 | async-start | bytes 10485760 | tf_op jit(solution)/shard_map/all_to_all | solution.py:31
  111.4 54.0 %all-gather.2.cloned.1.call-start = ((), (), s32[]{:S(2)}) async-start(), calls=%async_computation.5 | async-start | bytes 5242880 | tf_op jit(solution)/shard_map/all_gather | solution.py:28
  112.1 492.6 %reduce-scatter.3.cloned.1.call-start = ((), (), s32[]{:S(2)}) async-start(), calls=%async_computation.6 | async-start | bytes 11141120 | tf_op jit(solution)/shard_map/reduce_scatter | solution.py:40
  361.4 396.3 %copy-start.2 = (f32[1,5,16,256]{3,2,1,0:T(8,128)S(1)}, f32[1,5,16,256]{3,2,1,0:T(8,128)}, u32[]{:S(2)}) copy-start(f32[1,5,16,256]{3,2,1,0:T(8,128)} %param.4) | copy-start | bytes 245764
  361.4 304.5 %reduce-scatter.5.cloned.1.call-start = ((), (), s32[]{:S(2)}) async-start(), calls=%async_computation.7 | async-start | bytes 737280 | tf_op jit(solution)/shard_map/reduce_scatter | solution.py:41
  665.9 91.7 %copy-start.1 = (f32[1,5,16,256]{3,2,1,0:T(8,128)S(1)}, f32[1,5,16,256]{3,2,1,0:T(8,128)}, u32[]{:S(2)}) copy-start(f32[1,5,16,256]{3,2,1,0:T(8,128)} %reduce-scatter.5.cloned.1.call-done) | copy-start | bytes 245764
  668.3 29.2 %all-to-all-start.2 = ((f32[16,1,1280]{2,1,0:T(1,128)}), f32[16,1,1280]{2,1,0:T(1,128)S(1)}, u32[]{:S(2)}, u32[]{:S(2)}) async-start(f32[16,1,1280]{2,1,0:T(1,128)} %reshape.319), calls=%async_computation.4 | async-start | bytes 163840 | tf_op jit(solution)/shard_map/all_to_all | solution.py:42
  700.5 15.0 %collective-permute-start = (f32[5,16,256]{2,1,0:T(8,128)S(1)}, f32[5,16,256]{2,1,0:T(8,128)S(1)}, u32[]{:S(2)}, u32[]{:S(2)}) collective-permute-start(f32[5,16,256]{2,1,0:T(8,128)S(1)} %gather_fusion.1), channel_id=1, source_target_pairs={{16,0},{32,16},{48,32},{64,48},{80,64},{96,80},{112,96},{128,112},... | collective-permute-start | bytes 245768 | tf_op jit(solution)/shard_map/ppermute | solution.py:50
  715.6 14.2 %collective-permute-start.1 = (f32[5,16,256]{2,1,0:T(8,128)S(1)}, f32[5,16,256]{2,1,0:T(8,128)S(1)}, u32[]{:S(2)}, u32[]{:S(2)}) collective-permute-start(f32[5,16,256]{2,1,0:T(8,128)S(1)} %broadcast_select_fusion), channel_id=1, source_target_pairs={{32,0},{48,16},{64,32},{80,48},{96,64},{112,80},{128,96},{144,112}... | collective-permute-start | bytes 245768 | tf_op jit(solution)/shard_map/ppermute | solution.py:50
  729.8 12.3 %collective-permute-start.2 = (f32[5,16,256]{2,1,0:T(8,128)S(1)}, f32[5,16,256]{2,1,0:T(8,128)S(1)}, u32[]{:S(2)}, u32[]{:S(2)}) collective-permute-start(f32[5,16,256]{2,1,0:T(8,128)S(1)} %broadcast_select_fusion.1), channel_id=1, source_target_pairs={{64,0},{80,16},{96,32},{112,48},{128,64},{144,80},{160,96},{176,11... | collective-permute-start | bytes 245768 | tf_op jit(solution)/shard_map/ppermute | solution.py:50
  742.2 7.5 collective-permute-start.3
  749.9 7.8 %collective-permute-start.4 = (f32[5,16,256]{2,1,0:T(8,128)S(1)}, f32[5,16,256]{2,1,0:T(8,128)S(1)}, u32[]{:S(2)}, u32[]{:S(2)}) collective-permute-start(f32[5,16,256]{2,1,0:T(8,128)S(1)} %broadcast_select_fusion.3), channel_id=1, source_target_pairs={{256,0},{272,16},{288,32},{304,48},{320,64},{336,80},{352,96},{368... | collective-permute-start | bytes 245768 | tf_op jit(solution)/shard_map/ppermute | solution.py:50
Sparse Core Ops, SparseCore 0:
  114.3 51.0 all-gather.1
  361.5 243.0 reduce-scatter.2
  607.7 58.2 reduce-scatter.4
